TPU v7x, 256 devices: a whole 4x4x8 slice. The times are simulated.
256 devices in a mesh: section: 2 (over z_hi), dp: 16 (over z_lo, y), tensor: 8 (over x, core).
Axes of the slice: x: 4, y: 4, z: 8 (z_hi: 2, z_lo: 4; z = z_hi * 4 + z_lo), core: 2. Of those that a mesh axis runs over, the one named last changes fastest.
Arguments:
- section_input: bfloat16 [2, 1024, 8192], P('section', 'tensor', 'dp'), may hold values from -40 to 40
- norm_gain_attn: bfloat16 [2, 8192], P('section', 'dp'), may hold values from 0.099609375 to 1.8984375
- w_query: bfloat16 [2, 8192, 4096], P('section', 'dp', 'tensor'), may hold values from -0.0625 to 0.0625
- key_value_weight: bfloat16 [2, 2, 8192, 512], P('section', None, 'dp'), may hold values from -0.0625 to 0.0625
- w_output: bfloat16 [2, 4096, 8192], P('section', 'tensor', 'dp'), may hold values from -0.09375 to 0.09375
- norm_gain_ffn: bfloat16 [2, 8192], P('section', 'dp'), may hold values from 0.099609375 to 1.8984375
- w_gate_up: bfloat16 [2, 2, 8192, 14336], P('section', None, 'dp', 'tensor'), may hold values from -0.0625 to 0.0625
- w_down: bfloat16 [2, 14336, 8192], P('section', 'tensor', 'dp'), may hold values from -0.046875 to 0.046875
Outputs:
- section_output: bfloat16 [2, 1024, 8192], P('section', 'tensor', 'dp')
All inputs are finite; a program needn't handle non-finite values.
Results may differ from a plain program's by a relative error of at most 0.019.
Values may be sent and summed in bfloat16 or wider, within the bound.
A program may use at most 64 MiB of HBM per device.

v0:
```python
import math
import jax
import jax.numpy as jnp
from jax import lax
from jax.sharding import PartitionSpec as P

HEAD_SIZE = 128
QUERY_HEADS = 32
KEY_VALUE_HEADS = 4
EPS = 1e-05
THETA = 500000.0


def from_behind(x, axis, by):
    count = lax.axis_size(axis)
    return lax.ppermute(x, axis, [(i, (i + by) % count) for i in range(count)])


def apply_rotary(value_states, token_positions):
    width = value_states.shape[-1]
    half = width // 2
    freqs = jnp.exp(-(2.0 * jnp.arange(half, dtype=jnp.float32) / width) * math.log(THETA))
    angles = token_positions.astype(jnp.float32)[:, None] * freqs[None, :]
    cosine = jnp.cos(angles)[:, None, :]
    sine = jnp.sin(angles)[:, None, :]
    first = value_states[..., :half]
    second = value_states[..., half:]
    return jnp.concatenate(
        [first * cosine - second * sine, second * cosine + first * sine], axis=-1
    )


def local(
    section_input,
    norm_gain_attn,
    w_query,
    key_value_weight,
    w_output,
    norm_gain_ffn,
    w_gate_up,
    w_down,
):
    tile = section_input[0]
    rows_dev = tile.shape[0]
    cols_dev = tile.shape[1]
    tensor_count = lax.axis_size("tensor")
    data_count = lax.axis_size("dp")
    seq_total = rows_dev * tensor_count
    query_rows = seq_total // data_count
    width_total = cols_dev * data_count
    head_dim = HEAD_SIZE
    heads_dev = w_query.shape[2] // head_dim
    group_heads = QUERY_HEADS // KEY_VALUE_HEADS
    kv_dev = max(1, heads_dev // group_heads)
    per_kv = heads_dev // kv_dev
    tensor_pos = lax.axis_index("tensor")
    data_pos = lax.axis_index("dp")
    kv_first = tensor_pos * heads_dev // group_heads
    key_cols = lax.dynamic_slice_in_dim(
        key_value_weight[0], kv_first * head_dim, kv_dev * head_dim, 2
    )
    w_columns = jnp.concatenate([w_query[0], key_cols[0], key_cols[1]], axis=1)
    gain_attn = norm_gain_attn[0].astype(jnp.float32)[None, :]
    gain_ffn = norm_gain_ffn[0].astype(jnp.float32)[None, :]
    query_cols = heads_dev * head_dim
    kv_cols = kv_dev * head_dim
    query_pos = data_pos * query_rows + jnp.arange(query_rows, dtype=jnp.int32)
    all_pos = jnp.arange(seq_total, dtype=jnp.int32)
    arrived = from_behind(tile, "section", 1)
    wide = arrived.astype(jnp.float32)
    squares = lax.psum(jnp.sum(wide * wide, axis=1), "dp")
    normed_input = (wide * lax.rsqrt(squares / width_total + EPS)[:, None] * gain_attn).astype(
        jnp.bfloat16
    )
    partial_qkv = jnp.dot(
        lax.all_gather(normed_input, "tensor", axis=0, tiled=True),
        w_columns,
        preferred_element_type=jnp.float32,
    )
    query_sum = lax.psum_scatter(
        partial_qkv[:, :query_cols].astype(jnp.bfloat16), "dp", scatter_dimension=0, tiled=True
    ).astype(jnp.float32)
    key_sum = lax.psum(partial_qkv[:, query_cols:].astype(jnp.bfloat16), "dp").astype(jnp.float32)
    keys = apply_rotary(key_sum[:, :kv_cols].reshape(seq_total, kv_dev, head_dim), all_pos).astype(
        jnp.bfloat16
    )
    value_states = key_sum[:, kv_cols:].reshape(seq_total, kv_dev, head_dim).astype(jnp.bfloat16)
    query_states = apply_rotary(
        query_sum.reshape(query_rows, heads_dev, head_dim), query_pos
    ).astype(jnp.bfloat16)
    grouped = query_states.reshape(query_rows, kv_dev, per_kv, head_dim)
    scores = jnp.einsum(
        "qkgd,skd->kgqs", grouped, keys, preferred_element_type=jnp.float32
    ) * head_dim ** (-0.5)
    visible = all_pos[None, :] <= query_pos[:, None]
    weights_exp = jnp.where(visible, jnp.exp(scores), 0.0)
    probs = (weights_exp / jnp.sum(weights_exp, axis=-1, keepdims=True)).astype(jnp.bfloat16)
    mixed = (
        jnp.einsum("kgqs,skd->qkgd", probs, value_states, preferred_element_type=jnp.float32)
        .astype(jnp.bfloat16)
        .reshape(query_rows, query_cols)
    )
    attn_partial = jnp.dot(
        lax.all_gather(mixed, "dp", axis=0, tiled=True),
        w_output[0],
        preferred_element_type=jnp.float32,
    )
    attn = lax.psum_scatter(
        attn_partial.astype(jnp.bfloat16), "tensor", scatter_dimension=0, tiled=True
    ).astype(jnp.float32)
    resid = (arrived.astype(jnp.float32) + attn).astype(jnp.bfloat16)
    resid_wide = resid.astype(jnp.float32)
    squares_ffn = lax.psum(jnp.sum(resid_wide * resid_wide, axis=1), "dp")
    normed_ffn = (
        resid_wide * lax.rsqrt(squares_ffn / width_total + EPS)[:, None] * gain_ffn
    ).astype(jnp.bfloat16)
    rows_ffn = lax.all_gather(normed_ffn, "tensor", axis=0, tiled=True)
    ff_dev = w_gate_up.shape[3]
    summed = lax.psum_scatter(
        jnp.einsum("rd,gdf->rgf", rows_ffn, w_gate_up[0], preferred_element_type=jnp.float32)
        .reshape(query_rows * lax.axis_size("dp"), 2 * ff_dev)
        .astype(jnp.bfloat16),
        "dp",
        scatter_dimension=0,
        tiled=True,
    ).astype(jnp.float32)
    hidden = (jax.nn.silu(summed[:, :ff_dev]) * summed[:, ff_dev:]).astype(jnp.bfloat16)
    ffn_partial = jnp.dot(
        lax.all_gather(hidden, "dp", axis=0, tiled=True),
        w_down[0],
        preferred_element_type=jnp.float32,
    )
    ffn = lax.psum_scatter(
        ffn_partial.astype(jnp.bfloat16), "tensor", scatter_dimension=0, tiled=True
    ).astype(jnp.float32)
    result = (resid_wide + ffn).astype(jnp.bfloat16)
    return result[None]


def solution(mesh):
    placed = (
        P("section", "tensor", "dp"),
        P("section", "dp"),
        P("section", "dp", "tensor"),
        P("section", None, "dp", None),
        P("section", "tensor", "dp"),
        P("section", "dp"),
        P("section", None, "dp", "tensor"),
        P("section", "tensor", "dp"),
    )
    return jax.shard_map(
        local, mesh=mesh, in_specs=placed, out_specs=P("section", "tensor", "dp"), check_vma=False
    )
```

profile of v0, /device:TPU:8, one launch (start us, length us, event | category | flops | bytes accessed | tf_op | source)
XLA Modules:
  0.0 766.1 jit_solution(4502816704359785971)
XLA Ops:
  6.5 0.0 copy-start
  6.5 0.0 all-gather.5.cloned.1.call-start
  6.5 7.2 collective-permute-start
  13.7 0.7 mul.231
  14.4 3.1 collective-permute-done
  17.5 0.1 fusion.25
  17.6 38.6 %psum.21 = f32[128]{0:T(128)S(1)} all-reduce(f32[128]{0:T(128)S(1)} %fusion.25), channel_id=1, replica_groups=mesh['section'=2,'dp'=16,'tensor'=8] {'dp'}, use_global_device_ids=true, to_apply=%region_1.2 | all-reduce | flops 128 | bytes 1024 | tf_op jit(solution)/shard_map/psum | solution.py:71
  56.2 0.8 fusion.27
  57.0 0.0 all-gather.5.cloned.1.call-update
  57.0 0.0 all-reduce.2.cloned.1.call-start
  57.1 1.7 dynamic-slice_bitcast_fusion.1
  58.8 27.4 %all-gather.5.cloned.1.call-done = bf16[1024,512]{1,0:T(8,128)(2,1)} async-done(((bf16[128,512]{1,0:T(8,128)(2,1)}), bf16[1024,512]{1,0:T(8,128)(2,1)}) %all-gather.5.cloned.1.call-update) | async-done | bytes 1048592 | tf_op jit(solution)/shard_map/all_gather | solution.py:76
  86.2 2.4 convolution_convert_fusion.1
  88.7 0.8 slice.54
  89.5 0.0 all-reduce.2.cloned.1.call-update
  89.5 0.0 reduce-scatter.5.cloned.1.call-start
  89.6 1.0 slice.59
  90.6 0.0 reduce-scatter.5.cloned.1.call-update
  90.7 0.0 all-gather.7.cloned.1.call-start
  90.8 0.1 iota_compare_fusion
  90.9 0.2 multiply_cosine_fusion.1
  91.1 160.4 %all-reduce.2.cloned.1.call-done = bf16[1024,256]{1,0:T(8,128)(2,1)} async-done(((bf16[1024,256]{1,0:T(8,128)(2,1)}), bf16[1024,256]{1,0:T(8,128)(2,1)}) %all-reduce.2.cloned.1.call-update) | async-done | bytes 524304 | tf_op jit(solution)/shard_map/psum | solution.py:83
  251.5 1.1 fusion.33
  252.6 2.4 fusion.37
  255.0 79.3 %reduce-scatter.5.cloned.1.call-done = bf16[64,512]{1,0:T(8,128)(2,1)} async-done(((bf16[1024,512]{1,0:T(8,128)(2,1)}), bf16[64,512]{1,0:T(8,128)(2,1)}) %reduce-scatter.5.cloned.1.call-update) | async-done | bytes 65552 | tf_op jit(solution)/shard_map/reduce_scatter | solution.py:80
  334.3 0.9 reshape.220
  335.2 0.1 fusion.45
  335.4 0.6 fusion.46
  336.0 0.0 copy-done.2
  336.0 0.4 fusion.8
  336.3 0.0 copy-start.3
  336.4 0.1 copy.13
  336.4 0.6 copy.23
  337.1 0.0 all-gather.7.cloned.1.call-update
  337.1 0.0 reduce-scatter.7.cloned.1.call-start
  337.1 81.5 %all-gather.7.cloned.1.call-done = bf16[1024,512]{1,0:T(8,128)(2,1)} async-done(((bf16[64,512]{1,0:T(8,128)(2,1)}), bf16[1024,512]{1,0:T(8,128)(2,1)}) %all-gather.7.cloned.1.call-update) | async-done | bytes 1048592 | tf_op jit(solution)/shard_map/all_gather | solution.py:104
  418.6 3.0 convolution_convert_fusion.2
  421.7 0.0 reduce-scatter.7.cloned.1.call-update
  421.7 0.0 all-gather.9.cloned.1.call-start
  421.7 0.0 copy-done.3
  421.8 33.3 %reduce-scatter.7.cloned.1.call-done = bf16[128,512]{1,0:T(8,128)(2,1)} async-done(((bf16[1024,512]{1,0:T(8,128)(2,1)}), bf16[128,512]{1,0:T(8,128)(2,1)}) %reduce-scatter.7.cloned.1.call-update) | async-done | bytes 131088 | tf_op jit(solution)/shard_map/reduce_scatter | solution.py:108
  455.1 1.0 fusion.29
  456.1 39.0 %psum.23 = f32[128]{0:T(128)S(1)} all-reduce(f32[128]{0:T(128)S(1)} %fusion.29), channel_id=1, replica_groups=mesh['section'=2,'dp'=16,'tensor'=8] {'dp'}, use_global_device_ids=true, to_apply=%region_7.8 | all-reduce | flops 128 | bytes 1024 | tf_op jit(solution)/shard_map/psum | solution.py:113
  495.1 1.7 fusion.31
  496.7 0.0 all-gather.9.cloned.1.call-update
  496.7 0.0 reduce-scatter.9.cloned.1.call-start
  496.8 6.0 copy.14
  502.8 18.1 %all-gather.9.cloned.1.call-done = bf16[1024,512]{1,0:T(8,128)(2,1)} async-done(((bf16[128,512]{1,0:T(8,128)(2,1)}), bf16[1024,512]{1,0:T(8,128)(2,1)}) %all-gather.9.cloned.1.call-update) | async-done | bytes 1048592 | tf_op jit(solution)/shard_map/all_gather | solution.py:117
  520.9 9.3 %convolution_convert_fusion = bf16[1024,3584]{1,0:T(8,128)(2,1)} fusion(bf16[1024,512]{1,0:T(8,128)(2,1)} %all-gather.9.cloned.1.call-done, bf16[3584,512]{1,0:T(8,128)(2,1)} %bitcast.64), kind=kOutput, calls=%fused_computation | convolution fusion | flops 3761766400 | bytes 12058624 | tf_op jit(solution)/shard_map/rd,gdf->rgf/dot_general | solution.py:120
  530.2 0.0 reduce-scatter.9.cloned.1.call-update
  530.3 0.0 all-gather.11.cloned.1.call-start
  530.3 101.4 %reduce-scatter.9.cloned.1.call-done = bf16[64,3584]{1,0:T(8,128)(2,1)} async-done(((bf16[1024,3584]{1,0:T(8,128)(2,1)}), bf16[64,3584]{1,0:T(8,128)(2,1)}) %reduce-scatter.9.cloned.1.call-update) | async-done | bytes 458768 | tf_op jit(solution)/shard_map/reduce_scatter | solution.py:119
  631.7 1.1 convert_element_type.103
  632.8 0.8 fusion.24
  633.6 0.0 all-gather.11.cloned.1.call-update
  633.6 0.0 copy-start.1
  633.6 0.0 reduce-scatter.11.cloned.1.call-start
  633.7 85.8 %all-gather.11.cloned.1.call-done = bf16[1024,1792]{1,0:T(8,128)(2,1)} async-done(((bf16[64,1792]{1,0:T(8,128)(2,1)}), bf16[1024,1792]{1,0:T(8,128)(2,1)}) %all-gather.11.cloned.1.call-update) | async-done | bytes 3670032 | tf_op jit(solution)/shard_map/all_gather | solution.py:129
  719.4 0.0 copy-done
  719.4 5.1 fusion.2
  724.5 0.0 reduce-scatter.11.cloned.1.call-update
  724.5 33.5 %reduce-scatter.11.cloned.1.call-done = bf16[128,512]{1,0:T(8,128)(2,1)} async-done(((bf16[1024,512]{1,0:T(8,128)(2,1)}), bf16[128,512]{1,0:T(8,128)(2,1)}) %reduce-scatter.11.cloned.1.call-update) | async-done | bytes 131088 | tf_op jit(solution)/shard_map/reduce_scatter | solution.py:133
  758.0 0.0 copy-done.1
  758.0 1.6 fusion.38
  (9 shorter events, 0.1 us)
Async XLA Ops:
  6.5 712.9 %copy-start = (bf16[1,1792,512]{2,1,0:T(8,128)(2,1)S(1)}, bf16[1,1792,512]{2,1,0:T(8,128)(2,1)}, u32[]{:S(2)}) copy-start(bf16[1,1792,512]{2,1,0:T(8,128)(2,1)} %param.15) | copy-start | bytes 5505028
  6.5 79.7 %all-gather.5.cloned.1.call-start = ((), (), s32[]{:S(2)}) async-start(), calls=%async_computation.4 | async-start | bytes 1179648 | tf_op jit(solution)/shard_map/all_gather | solution.py:76
  6.5 11.0 %collective-permute-start = (bf16[128,512]{1,0:T(8,128)(2,1)}, bf16[128,512]{1,0:T(8,128)(2,1)S(1)}, u32[]{:S(2)}, u32[]{:S(2)}) collective-permute-start(bf16[128,512]{1,0:T(8,128)(2,1)} %bitcast.70), channel_id=1, source_target_pairs={{0,128},{128,0},{1,129},{129,1},{2,130},{130,2},{3,131},{131,3},{4... | collective-permute-start | bytes 393224 | tf_op jit(solution)/shard_map/ppermute | solution.py:16
  57.0 194.5 %all-reduce.2.cloned.1.call-start = ((), (), s32[]{:S(2)}) async-start(), calls=%async_computation.5 | async-start | bytes 1048576 | tf_op jit(solution)/shard_map/psum | solution.py:83
  89.5 244.8 %reduce-scatter.5.cloned.1.call-start = ((), (), s32[]{:S(2)}) async-start(), calls=%async_computation.6 | async-start | bytes 1114112 | tf_op jit(solution)/shard_map/reduce_scatter | solution.py:80
  90.7 328.0 %all-gather.7.cloned.1.call-start = ((), (), s32[]{:S(2)}) async-start(), calls=%async_computation.7 | async-start | bytes 1114112 | tf_op jit(solution)/shard_map/all_gather | solution.py:104
  251.5 84.5 %copy-start.2 = (bf16[1024,256]{1,0:T(8,128)(2,1)S(1)}, bf16[1024,256]{1,0:T(8,128)(2,1)}, u32[]{:S(2)}) copy-start(bf16[1024,256]{1,0:T(8,128)(2,1)} %all-reduce.2.cloned.1.call-done) | copy-start | bytes 1572868
  336.3 85.4 %copy-start.3 = (bf16[1,512]{1,0:T(2,128)(2,1)S(1)}, bf16[1,512]{1,0:T(2,128)(2,1)}, u32[]{:S(2)}) copy-start(bf16[1,512]{1,0:T(2,128)(2,1)} %param.13) | copy-start | bytes 3076
  337.1 118.0 %reduce-scatter.7.cloned.1.call-start = ((), (), s32[]{:S(2)}) async-start(), calls=%async_computation.8 | async-start | bytes 1179648 | tf_op jit(solution)/shard_map/reduce_scatter | solution.py:108
  421.7 99.2 %all-gather.9.cloned.1.call-start = ((), (), s32[]{:S(2)}) async-start(), calls=%async_computation.9 | async-start | bytes 1179648 | tf_op jit(solution)/shard_map/all_gather | solution.py:117
  496.7 134.9 %reduce-scatter.9.cloned.1.call-start = ((), (), s32[]{:S(2)}) async-start(), calls=%async_computation.10 | async-start | bytes 7798784 | tf_op jit(solution)/shard_map/reduce_scatter | solution.py:119
  530.3 189.1 %all-gather.11.cloned.1.call-start = ((), (), s32[]{:S(2)}) async-start(), calls=%async_computation.11 | async-start | bytes 3899392 | tf_op jit(solution)/shard_map/all_gather | solution.py:129
  633.6 124.4 %copy-start.1 = (bf16[128,512]{1,0:T(8,128)(2,1)S(1)}, bf16[128,512]{1,0:T(8,128)(2,1)}, u32[]{:S(2)}) copy-start(bf16[128,512]{1,0:T(8,128)(2,1)} %reduce-scatter.7.cloned.1.call-done) | copy-start | bytes 393220
  633.6 124.4 %reduce-scatter.11.cloned.1.call-start = ((), (), s32[]{:S(2)}) async-start(), calls=%async_computation.12 | async-start | bytes 1179648 | tf_op jit(solution)/shard_map/reduce_scatter | solution.py:133
Sparse Core Ops, SparseCore 0:
  57.2 29.0 all-gather.4
  89.7 161.8 all-reduce.1
  254.0 80.2 reduce-scatter.4
  337.2 81.3 all-gather.6
  421.8 33.1 reduce-scatter.6
  496.9 24.0 all-gather.8
  530.4 101.2 reduce-scatter.8
  633.7 85.6 all-gather.10
  724.7 33.2 reduce-scatter.10
where the time goes:
time: 767 us; the launch traced here: 766 us
  waiting for transfers between devices  624 us (81%)
  blocking collectives  77.6 us (10%)
  matrix products  20.8 us (3%)
  between operations  13.4 us (2%)
  other arithmetic  11.6 us (2%)
  local copies, waits for them, and re-layouts  11.3 us (1%)
    psum x1, waiting for transfers between devices, local(): lax.psum(partial_qkv[:, query_cols:].astype(jnp.bfloat16), 'dp')  160 us
    reduce_scatter x1, waiting for transfers between devices, local(): lax.psum_scatter(jnp.einsum('rd,gdf->rgf', rows_ffn, w_gate_up[0], prefer...  101 us
    all_gather x1, waiting for transfers between devices, local(): lax.all_gather(hidden, 'dp', axis=0, tiled=True)  85.8 us
    all_gather x1, waiting for transfers between devices, local(): lax.all_gather(mixed, 'dp', axis=0, tiled=True)  81.5 us
    reduce_scatter x1, waiting for transfers between devices, local(): lax.psum_scatter(partial_qkv[:, :query_cols].astype(jnp.bfloat16), 'dp',...  79.3 us
    psum x1, blocking collectives, local(): squares_ffn = lax.psum(jnp.sum(resid_wide * resid_wide, axis=1), 'dp')  39 us
    psum x1, blocking collectives, local(): squares = lax.psum(jnp.sum(wide * wide, axis=1), 'dp')  38.6 us
    reduce_scatter x1, waiting for transfers between devices, local(): lax.psum_scatter(ffn_partial.astype(jnp.bfloat16), 'tensor', scatter_dime...  33.5 us
  transfers between devices with their start and end apart: 10, of which 10 were waited for; matrix products, arithmetic and copies ran while one was open for 2% of the time, Pallas kernels for 0%

commit v1 on v0

--- a/solution.py
+++ b/solution.py
@@ -9,6 +9,28 @@
 KEY_VALUE_HEADS = 4
 EPS = 1e-05
 THETA = 500000.0
+
+
+def in_order(blocks, dim):
+    blocks = jnp.moveaxis(blocks, 0, dim)
+    lengths = blocks.shape
+    return blocks.reshape(*lengths[:dim], lengths[dim] * lengths[dim + 1], *lengths[dim + 2 :])
+
+
+def ring_gather(array, axis, dim):
+    count = lax.axis_size(axis)
+    pairs = [(i, (i + 1) % count) for i in range(count)]
+    back = [(b, a) for a, b in pairs]
+    lower, upper = ([], [])
+    for step in range(count - 1):
+        if step % 2 == 0:
+            lower.append(lax.ppermute(lower[-1] if lower else array, axis, pairs))
+        else:
+            upper.append(lax.ppermute(upper[-1] if upper else array, axis, back))
+    tiles = jnp.stack([*lower[::-1], array, *upper])
+    shift = lax.axis_index(axis) - len(lower)
+    tiles = tiles[(jnp.arange(count) - shift) % count]
+    return in_order(tiles, dim)
 
 
 def from_behind(x, axis, by):
@@ -73,9 +95,7 @@
         jnp.bfloat16
     )
     partial_qkv = jnp.dot(
-        lax.all_gather(normed_input, "tensor", axis=0, tiled=True),
-        w_columns,
-        preferred_element_type=jnp.float32,
+        ring_gather(normed_input, "tensor", 0), w_columns, preferred_element_type=jnp.float32
     )
     query_sum = lax.psum_scatter(
         partial_qkv[:, :query_cols].astype(jnp.bfloat16), "dp", scatter_dimension=0, tiled=True

time: 767 us -> 767 us (level)
  waiting for transfers between devices: 624 us -> 612 us
  starting transfers between devices: 7.53 us -> 16.4 us
    all_gather x1 -> x0, waiting for transfers between devices: 27.4 us -> none  [local(): lax.all_gather(normed_input, 'tensor', axis=0, tiled=True)]
    ppermute x0 -> x7, waiting for transfers between devices: none -> 11.9 us  [the longest x4 11.9 us: ring_gather(): lower.append(lax.ppermute(lower[-1] if lower else array, axis, pairs))]
    ppermute x0 -> x7, starting transfers between devices: none -> 8.87 us  [the longest x3 8.84 us: ring_gather(): upper.append(lax.ppermute(upper[-1] if upper else array, axis, back))]
  transfers between devices with their start and end apart: 10 -> 16, of which waited for: 10 -> 13; matrix products, arithmetic and copies ran while one was open for 2% -> 2% of each run, Pallas kernels for 0% -> 0%
where the time goes in v1:
time: 767 us; the launch traced here: 766 us
  waiting for transfers between devices  612 us (80%)
  blocking collectives  77.6 us (10%)
  matrix products  20.8 us (3%)
  starting transfers between devices  16.4 us (2%)
  local copies, waits for them, and re-layouts  14.7 us (2%)
  between operations  13.8 us (2%)
  other arithmetic  11.1 us (1%)
    psum x1, waiting for transfers between devices, local(): lax.psum(partial_qkv[:, query_cols:].astype(jnp.bfloat16), 'dp')  164 us
    reduce_scatter x1, waiting for transfers between devices, local(): lax.psum_scatter(jnp.einsum('rd,gdf->rgf', rows_ffn, w_gate_up[0], prefer...  102 us
    all_gather x1, waiting for transfers between devices, local(): lax.all_gather(hidden, 'dp', axis=0, tiled=True)  85.4 us
    all_gather x1, waiting for transfers between devices, local(): lax.all_gather(mixed, 'dp', axis=0, tiled=True)  81.5 us
    reduce_scatter x1, waiting for transfers between devices, local(): lax.psum_scatter(partial_qkv[:, :query_cols].astype(jnp.bfloat16), 'dp',...  79.3 us
    psum x1, blocking collectives, local(): squares_ffn = lax.psum(jnp.sum(resid_wide * resid_wide, axis=1), 'dp')  39 us
    psum x1, blocking collectives, local(): squares = lax.psum(jnp.sum(wide * wide, axis=1), 'dp')  38.6 us
    reduce_scatter x1, waiting for transfers between devices, local(): lax.psum_scatter(ffn_partial.astype(jnp.bfloat16), 'tensor', scatter_dime...  33.4 us
  transfers between devices with their start and end apart: 16, of which 13 were waited for; matrix products, arithmetic and copies ran while one was open for 2% of the time, Pallas kernels for 0%

profile of v1, /device:TPU:8, one launch (start us, length us, event | category | flops | bytes accessed | tf_op | source)
XLA Modules:
  0.0 766.1 jit_solution(2201508431720787685)
XLA Ops:
  6.5 7.2 collective-permute-start
  13.7 0.7 mul.231
  14.4 3.1 collective-permute-done
  17.5 0.1 fusion.25
  17.6 38.6 %psum.21 = f32[128]{0:T(128)S(1)} all-reduce(f32[128]{0:T(128)S(1)} %fusion.25), channel_id=1, replica_groups=mesh['section'=2,'dp'=16,'tensor'=8] {'dp'}, use_global_device_ids=true, to_apply=%region_1.2 | all-reduce | flops 128 | bytes 1024 | tf_op jit(solution)/shard_map/psum | solution.py:93
  56.2 0.1 fusion.27
  56.4 0.0 collective-permute-start.1
  56.4 5.6 collective-permute-done.1
  62.0 3.0 collective-permute-start.5
  64.9 2.6 collective-permute-done.2
  67.6 3.0 collective-permute-start.6
  70.6 2.6 collective-permute-done.3
  73.2 1.7 dynamic-slice_bitcast_fusion.1
  74.9 2.9 collective-permute-start.7
  77.8 1.1 collective-permute-done.4
  78.9 0.9 bitcast_dynamic-update-slice_fusion.7
  79.9 0.1 bitcast_dynamic-update-slice_fusion.3
  80.0 0.9 bitcast_dynamic-update-slice_fusion.1
  80.9 1.6 gather_fusion
  82.5 2.4 convolution_convert_fusion.1
  85.0 0.8 slice.56
  85.8 0.0 all-reduce.2.cloned.1.call-update
  85.8 0.0 reduce-scatter.5.cloned.1.call-start
  85.9 1.1 slice.61
  87.0 0.0 all-gather.4.cloned.1.call-start
  87.1 0.1 iota_compare_fusion
  87.2 0.2 multiply_cosine_fusion.1
  87.4 163.7 %all-reduce.2.cloned.1.call-done = bf16[1024,256]{1,0:T(8,128)(2,1)} async-done(((bf16[1024,256]{1,0:T(8,128)(2,1)}), bf16[1024,256]{1,0:T(8,128)(2,1)}) %all-reduce.2.cloned.1.call-update) | async-done | bytes 524304 | tf_op jit(solution)/shard_map/psum | solution.py:103
  251.1 1.1 fusion.33
  252.2 2.4 fusion.37
  254.6 79.3 %reduce-scatter.5.cloned.1.call-done = bf16[64,512]{1,0:T(8,128)(2,1)} async-done(((bf16[1024,512]{1,0:T(8,128)(2,1)}), bf16[64,512]{1,0:T(8,128)(2,1)}) %reduce-scatter.5.cloned.1.call-update) | async-done | bytes 65552 | tf_op jit(solution)/shard_map/reduce_scatter | solution.py:100
  333.9 0.9 reshape.273
  334.8 0.1 fusion.47
  335.0 0.6 fusion.48
  335.6 0.4 fusion.8
  336.0 0.1 copy.13
  336.0 0.6 copy.23
  336.7 0.0 all-gather.4.cloned.1.call-update
  336.7 0.0 reduce-scatter.7.cloned.1.call-start
  336.7 81.5 %all-gather.4.cloned.1.call-done = bf16[1024,512]{1,0:T(8,128)(2,1)} async-done(((bf16[64,512]{1,0:T(8,128)(2,1)}), bf16[1024,512]{1,0:T(8,128)(2,1)}) %all-gather.4.cloned.1.call-update) | async-done | bytes 1048592 | tf_op jit(solution)/shard_map/all_gather | solution.py:124
  418.2 3.0 convolution_convert_fusion.2
  421.3 0.0 reduce-scatter.7.cloned.1.call-update
  421.3 0.0 all-gather.6.cloned.1.call-start
  421.4 33.3 %reduce-scatter.7.cloned.1.call-done = bf16[128,512]{1,0:T(8,128)(2,1)} async-done(((bf16[1024,512]{1,0:T(8,128)(2,1)}), bf16[128,512]{1,0:T(8,128)(2,1)}) %reduce-scatter.7.cloned.1.call-update) | async-done | bytes 131088 | tf_op jit(solution)/shard_map/reduce_scatter | solution.py:128
  454.7 1.0 fusion.29
  455.7 39.0 %psum.23 = f32[128]{0:T(128)S(1)} all-reduce(f32[128]{0:T(128)S(1)} %fusion.29), channel_id=1, replica_groups=mesh['section'=2,'dp'=16,'tensor'=8] {'dp'}, use_global_device_ids=true, to_apply=%region_7.8 | all-reduce | flops 128 | bytes 1024 | tf_op jit(solution)/shard_map/psum | solution.py:133
  494.7 1.7 fusion.31
  496.4 0.0 all-gather.6.cloned.1.call-update
  496.4 0.0 reduce-scatter.9.cloned.1.call-start
  496.5 6.0 copy.14
  502.4 18.1 %all-gather.6.cloned.1.call-done = bf16[1024,512]{1,0:T(8,128)(2,1)} async-done(((bf16[128,512]{1,0:T(8,128)(2,1)}), bf16[1024,512]{1,0:T(8,128)(2,1)}) %all-gather.6.cloned.1.call-update) | async-done | bytes 1048592 | tf_op jit(solution)/shard_map/all_gather | solution.py:137
  520.5 9.3 %convolution_convert_fusion = bf16[1024,3584]{1,0:T(8,128)(2,1)} fusion(bf16[1024,512]{1,0:T(8,128)(2,1)} %all-gather.6.cloned.1.call-done, bf16[3584,512]{1,0:T(8,128)(2,1)} %bitcast.83), kind=kOutput, calls=%fused_computation.1 | convolution fusion | flops 3761766400 | bytes 12058624 | tf_op jit(solution)/shard_map/rd,gdf->rgf/dot_general | solution.py:140
  529.8 0.0 reduce-scatter.9.cloned.1.call-update
  529.9 0.0 all-gather.8.cloned.1.call-start
  529.9 101.8 %reduce-scatter.9.cloned.1.call-done = bf16[64,3584]{1,0:T(8,128)(2,1)} async-done(((bf16[1024,3584]{1,0:T(8,128)(2,1)}), bf16[64,3584]{1,0:T(8,128)(2,1)}) %reduce-scatter.9.cloned.1.call-update) | async-done | bytes 458768 | tf_op jit(solution)/shard_map/reduce_scatter | solution.py:139
  631.8 1.1 convert_element_type.103
  632.8 0.8 fusion.24
  633.7 0.0 all-gather.8.cloned.1.call-update
  633.7 0.0 reduce-scatter.11.cloned.1.call-start
  633.8 85.4 %all-gather.8.cloned.1.call-done = bf16[1024,1792]{1,0:T(8,128)(2,1)} async-done(((bf16[64,1792]{1,0:T(8,128)(2,1)}), bf16[1024,1792]{1,0:T(8,128)(2,1)}) %all-gather.8.cloned.1.call-update) | async-done | bytes 3670032 | tf_op jit(solution)/shard_map/all_gather | solution.py:149
  719.1 5.1 fusion.2
  724.2 0.0 reduce-scatter.11.cloned.1.call-update
  724.2 33.4 %reduce-scatter.11.cloned.1.call-done = bf16[128,512]{1,0:T(8,128)(2,1)} async-done(((bf16[1024,512]{1,0:T(8,128)(2,1)}), bf16[128,512]{1,0:T(8,128)(2,1)}) %reduce-scatter.11.cloned.1.call-update) | async-done | bytes 131088 | tf_op jit(solution)/shard_map/reduce_scatter | solution.py:153
  757.6 1.6 fusion.38
  (31 shorter events, 0.2 us)
Async XLA Ops:
  6.5 712.6 %copy-start = (bf16[1,1792,512]{2,1,0:T(8,128)(2,1)S(1)}, bf16[1,1792,512]{2,1,0:T(8,128)(2,1)}, u32[]{:S(2)}) copy-start(bf16[1,1792,512]{2,1,0:T(8,128)(2,1)} %param.15) | copy-start | bytes 5505028
  6.5 244.6 %all-reduce.2.cloned.1.call-start = ((), (), s32[]{:S(2)}) async-start(), calls=%async_computation.4 | async-start | bytes 1048576 | tf_op jit(solution)/shard_map/psum | solution.py:103
  6.5 11.0 %collective-permute-start = (bf16[128,512]{1,0:T(8,128)(2,1)}, bf16[128,512]{1,0:T(8,128)(2,1)S(1)}, u32[]{:S(2)}, u32[]{:S(2)}) collective-permute-start(bf16[128,512]{1,0:T(8,128)(2,1)} %bitcast.91), channel_id=1, source_target_pairs={{0,128},{128,0},{1,129},{129,1},{2,130},{130,2},{3,131},{131,3},{4... | collective-permute-start | bytes 393224 | tf_op jit(solution)/shard_map/ppermute | solution.py:38
  56.4 5.6 collective-permute-start.1
  62.0 5.6 collective-permute-start.2
  62.0 5.6 collective-permute-start.5
  67.6 5.6 collective-permute-start.3
  67.6 7.3 collective-permute-start.6
  73.2 5.7 collective-permute-start.4
  74.9 6.0 collective-permute-start.7
  85.8 248.1 %reduce-scatter.5.cloned.1.call-start = ((), (), s32[]{:S(2)}) async-start(), calls=%async_computation.5 | async-start | bytes 1114112 | tf_op jit(solution)/shard_map/reduce_scatter | solution.py:100
  87.0 331.3 %all-gather.4.cloned.1.call-start = ((), (), s32[]{:S(2)}) async-start(), calls=%async_computation.6 | async-start | bytes 1114112 | tf_op jit(solution)/shard_map/all_gather | solution.py:124
  251.1 84.5 %copy-start.2 = (bf16[1024,256]{1,0:T(8,128)(2,1)S(1)}, bf16[1024,256]{1,0:T(8,128)(2,1)}, u32[]{:S(2)}) copy-start(bf16[1024,256]{1,0:T(8,128)(2,1)} %all-reduce.2.cloned.1.call-done) | copy-start | bytes 1572868
  335.9 85.4 %copy-start.3 = (bf16[1,512]{1,0:T(2,128)(2,1)S(1)}, bf16[1,512]{1,0:T(2,128)(2,1)}, u32[]{:S(2)}) copy-start(bf16[1,512]{1,0:T(2,128)(2,1)} %param.13) | copy-start | bytes 3076
  336.7 118.0 %reduce-scatter.7.cloned.1.call-start = ((), (), s32[]{:S(2)}) async-start(), calls=%async_computation.7 | async-start | bytes 1179648 | tf_op jit(solution)/shard_map/reduce_scatter | solution.py:128
  421.3 99.2 %all-gather.6.cloned.1.call-start = ((), (), s32[]{:S(2)}) async-start(), calls=%async_computation.8 | async-start | bytes 1179648 | tf_op jit(solution)/shard_map/all_gather | solution.py:137
  496.4 135.3 %reduce-scatter.9.cloned.1.call-start = ((), (), s32[]{:S(2)}) async-start(), calls=%async_computation.9 | async-start | bytes 7798784 | tf_op jit(solution)/shard_map/reduce_scatter | solution.py:139
  529.9 189.3 %all-gather.8.cloned.1.call-start = ((), (), s32[]{:S(2)}) async-start(), calls=%async_computation.10 | async-start | bytes 3899392 | tf_op jit(solution)/shard_map/all_gather | solution.py:149
  633.7 123.9 %copy-start.1 = (bf16[128,512]{1,0:T(8,128)(2,1)S(1)}, bf16[128,512]{1,0:T(8,128)(2,1)}, u32[]{:S(2)}) copy-start(bf16[128,512]{1,0:T(8,128)(2,1)} %reduce-scatter.7.cloned.1.call-done) | copy-start | bytes 393220
  633.7 123.9 %reduce-scatter.11.cloned.1.call-start = ((), (), s32[]{:S(2)}) async-start(), calls=%async_computation.11 | async-start | bytes 1179648 | tf_op jit(solution)/shard_map/reduce_scatter | solution.py:153
Sparse Core Ops, SparseCore 0:
  86.0 165.1 all-reduce.1
  253.6 80.2 reduce-scatter.4
  336.8 81.3 all-gather.3
  421.4 33.1 reduce-scatter.6
  496.5 23.9 all-gather.5
  530.0 101.7 reduce-scatter.8
  633.8 85.2 all-gather.7
  724.4 33.1 reduce-scatter.10
